TPU v7x, 32 devices: a whole 2x2x4 slice. The times are simulated.
32 devices in a mesh: dp: 4 (over y, core), seq: 8 (over z, x).
Axes of the slice: x: 2, y: 2, z: 4, core: 2. Of those that a mesh axis runs over, the one named last changes fastest.
Arguments:
- tokens: bfloat16 [4, 24, 256, 1280], P('dp', 'seq'), may hold values from -6 to 6
- clip_ids: int32 [4, 24], P('dp'), may hold values from 0 to 5, never falling along the last dimension, each value on 1 to 12 neighbouring positions
- ln_gain: float32 [1280], replicated, may hold values from 0.1 to 1.9
- w_qkv: bfloat16 [1280, 1920], P(None, 'dp'), may hold values from -0.15625 to 0.15625
- w_out: bfloat16 [640, 1280], P(None, 'dp'), may hold values from -0.25 to 0.25
Outputs:
- output: bfloat16 [4, 24, 256, 1280], P('dp', 'seq')
Inputs may be any that keep to these rules, and one draw needn't show every extreme that they name: `clip_ids`: in each batch the clip numbers never fall along the frames, every clip number occurs, each clip covers 1 to 12 consecutive frames, and some clip covers exactly 12.
All inputs are finite; a program needn't handle non-finite values.
Results may differ from a plain program's by a relative error of at most 0.006.
Values may be sent and summed in bfloat16 or wider, within the bound.
A program may use at most 64 MiB of HBM per device.

v0:
```python
import math
import jax
import jax.numpy as jnp
from jax import lax
from jax.sharding import PartitionSpec as P

HS = 80
HEADS = 8
HD = 640
norm_eps = 1e-05


def layer_norm(block, ln_gain):
    values = block.astype(jnp.float32)
    center = jnp.mean(values, axis=-1, keepdims=True)
    spread = jnp.mean(jnp.square(values - center), axis=-1, keepdims=True)
    return ((values - center) * lax.rsqrt(spread + norm_eps) * ln_gain).astype(jnp.bfloat16)


def split_heads(projected):
    queries = (projected[:, :HD] * (1.0 / math.sqrt(HS))).astype(jnp.bfloat16)
    keys = projected[:, HD : 2 * HD].astype(jnp.bfloat16)
    values = projected[:, 2 * HD :].astype(jnp.bfloat16)
    return (queries, keys, values)


def attend(queries, keys, values, clip_row):
    scores = jnp.einsum("flhe,glhe->lhfg", queries, keys, preferred_element_type=jnp.float32)
    same_clip = clip_row[:, None] == clip_row[None, :]
    raised = jnp.where(same_clip, jnp.exp(scores), jnp.zeros_like(scores))
    attn_probs = (raised / jnp.sum(raised, axis=-1, keepdims=True)).astype(jnp.bfloat16)
    return jnp.einsum(
        "lhfg,glhe->flhe", attn_probs, values, preferred_element_type=jnp.float32
    ).astype(jnp.bfloat16)


def shards(tokens, clip_ids, ln_gain, w_qkv, w_out):
    width = tokens.shape[3]
    clip_row = clip_ids[0]
    frames = clip_row.shape[0]
    local_frames = tokens.shape[1]
    patches = tokens.shape[2]
    moved = lax.all_to_all(tokens, "seq", split_axis=2, concat_axis=1, tiled=True)
    places = moved.shape[2]
    normed = layer_norm(moved, ln_gain).reshape(frames * places, width)

    def column_block(piece, start):
        return jnp.dot(normed, piece, preferred_element_type=jnp.float32)

    queries, keys, values = split_heads(
        column_block(lax.all_gather(w_qkv, "dp", axis=1, tiled=True), jnp.int32(0))
    )
    head_shape = (frames, places, HEADS, HS)
    mixed = attend(
        queries.reshape(head_shape), keys.reshape(head_shape), values.reshape(head_shape), clip_row
    )
    mixed = lax.all_to_all(
        mixed.reshape(1, frames, places, HD), "seq", split_axis=1, concat_axis=2, tiled=True
    )
    row_count = local_frames * patches
    rows_in = mixed.reshape(row_count, HD)

    def column_block(piece, start):
        return jnp.dot(rows_in, piece, preferred_element_type=jnp.float32)

    update = column_block(lax.all_gather(w_out, "dp", axis=1, tiled=True), jnp.int32(0))
    summed = tokens.reshape(row_count, width).astype(jnp.float32) + update
    return summed.astype(jnp.bfloat16).reshape(tokens.shape)


def solution(mesh):
    placed = (P("dp", "seq", None, None), P("dp", None), P(), P(None, "dp"), P(None, "dp"))
    return jax.shard_map(
        shards, mesh=mesh, in_specs=placed, out_specs=P("dp", "seq", None, None), check_vma=False
    )
```

profile of v0, /device:TPU:0, one launch (start us, length us, event | category | flops | bytes accessed | tf_op | source)
XLA Modules:
  0.0 151.9 jit_solution(18149255715372341711)
XLA Ops:
  6.5 0.0 all-gather.3.cloned.1.call-start
  6.5 0.7 all-gather.3.cloned.1.call-update
  7.3 4.8 %copy.35 = bf16[1,3,256,1280]{3,1,0,2:T(4,128)(2,1)} copy(bf16[1,3,256,1280]{3,2,1,0:T(8,128)(2,1)} %param.5) | data formatting | bytes 3932160 | tf_op args[0]
  12.0 0.0 copy-start.2
  12.0 7.4 %all-to-all-start = ((bf16[1,3,256,1280]{3,1,0,2:T(4,128)(2,1)}), bf16[1,3,256,1280]{3,1,0,2:T(4,128)(2,1)S(1)}, u32[]{:S(2)}, u32[]{:S(2)}) async-start(bf16[1,3,256,1280]{3,1,0,2:T(4,128)(2,1)} %copy.35), calls=%async_computation | async-start | bytes 5242880 | tf_op jit(solution)/shard_map/all_to_all | solution.py:43
  19.4 0.0 all-gather.5.cloned.1.call-start
  19.5 0.7 all-gather.5.cloned.1.call-update
  20.2 0.0 copy-done.2
  20.2 0.1 broadcast_compare_fusion
  20.3 58.6 %all-to-all-done = bf16[1,3,256,1280]{3,1,0,2:T(4,128)(2,1)S(1)} async-done(((bf16[1,3,256,1280]{3,1,0,2:T(4,128)(2,1)}), bf16[1,3,256,1280]{3,1,0,2:T(4,128)(2,1)S(1)}, u32[]{:S(2)}, u32[]{:S(2)}) %all-to-all-start) | async-done | bytes 1966112 | tf_op jit(solution)/shard_map/all_to_all | solution.py:43
  78.9 2.3 %convert_bitcast_fusion = (f32[1,8,3,32,1280]{4,3,1,2,0:T(8,128)}, bf16[1,3,256,1280]{3,2,1,0:T(8,128)(2,1)S(1)}) fusion(bf16[1,3,256,1280]{3,1,0,2:T(4,128)(2,1)S(1)} %all-to-all-done), kind=kLoop, calls=%fused_computation.1 | loop fusion | flops 983040 | bytes 7864320 | tf_op jit(solution)/shard_map/convert_element_type | solution.py:14
  81.2 0.3 fusion.5
  81.6 0.7 multiply_reduce_fusion
  82.3 0.1 rsqrt.12
  82.4 0.1 div.17
  82.4 0.0 copy-start.1
  82.4 2.4 %copy.37 = f32[1,8,3,32,1280]{4,3,2,1,0:T(8,128)S(1)} copy(f32[1,8,3,32,1280]{4,3,1,2,0:T(8,128)} %get-tuple-element.5) | data formatting | bytes 7864320 | tf_op jit(solution)/shard_map/convert_element_type | solution.py:14
  84.9 0.0 copy-done.1
  84.9 0.6 fusion.2
  85.4 0.0 all-gather.3.cloned.1.call-done
  85.5 8.5 %fusion.18 = (bf16[768,1920]{1,0:T(8,128)(2,1)S(1)}, f32[768,1920]{1,0:T(8,128)}) fusion(bf16[768,1280]{1,0:T(8,128)(2,1)S(1)} %fusion.2, bf16[1280,1920]{0,1:T(8,128)(2,1)} %all-gather.3.cloned.1.call-done), kind=kOutput, calls=%fused_computation.27 | convolution fusion | flops 3776348160 | bytes 15728640 | tf_op jit(solution)/shard_map/dot_general | solution.py:48
  94.0 0.2 fusion.17
  94.2 1.6 %reshape.90 = bf16[24,32,8,80]{3,2,1,0:T(8,128)(2,1)S(1)} reshape(bf16[768,640]{1,0:T(8,128)(2,1)S(1)} %get-tuple-element.8) | data formatting | bytes 1966080 | tf_op jit(solution)/shard_map/reshape | solution.py:55
  95.8 1.7 %fusion.6 = bf16[768,640]{1,0:T(8,128)(2,1)S(1)} fusion(f32[768,1920]{1,0:T(8,128)} %get-tuple-element.10), kind=kLoop, calls=%fused_computation.13 | loop fusion | flops 983040 | bytes 2949120 | tf_op jit(solution)/shard_map/convert_element_type | solution.py:21
  97.5 2.5 %reshape.89 = bf16[24,32,8,80]{3,2,1,0:T(8,128)(2,1)} reshape(bf16[768,640]{1,0:T(8,128)(2,1)S(1)} %fusion.6) | data formatting | bytes 1966080 | tf_op jit(solution)/shard_map/reshape | solution.py:55
  100.0 5.7 %fusion.4 = (f32[32,8,24]{2,1,0:T(8,128)S(1)}, f32[32,8,24,24]{2,3,1,0:T(8,128)}) fusion(pred[24,24]{0,1:T(8,128)(4,1)S(1)} %broadcast_compare_fusion, bf16[24,32,8,80]{3,2,1,0:T(8,128)(2,1)S(1)} %reshape.90, bf16[24,32,8,80]{3,2,1,0:T(8,128)(2,1)} %reshape.89), kind=kOutput, calls=%fused_computation.10 | convolution fusion | flops 23881728 | bytes 2581056 | tf_op jit(solution)/shard_map/flhe,glhe->lhfg/dot_general | solution.py:28
  105.7 1.6 %reshape.88 = bf16[24,32,8,80]{3,2,1,0:T(8,128)(2,1)S(1)} reshape(bf16[768,640]{1,0:T(8,128)(2,1)S(1)} %get-tuple-element.7) | data formatting | bytes 1966080 | tf_op jit(solution)/shard_map/reshape | solution.py:55
  107.3 3.4 %fusion.13 = bf16[24,32,8,80]{3,0,2,1:T(8,128)(2,1)S(1)} fusion(f32[32,8,24,24]{2,3,1,0:T(8,128)} %get-tuple-element.12, f32[32,8,24]{2,1,0:T(8,128)S(1)} %get-tuple-element.11, pred[24,24]{0,1:T(8,128)(4,1)S(1)} %broadcast_compare_fusion, bf16[24,32,8,80]{3,2,1,0:T(8,128)(2,1)S(1)} %reshape.88), kind=kOutput, calls=%fused_computation.21 | convolution fusion | flops 24526848 | bytes 2581056 | tf_op jit(solution)/shard_map/lhfg,glhe->flhe/dot_general | solution.py:32
  110.7 0.3 copy.44
  111.1 1.2 reshape.91
  112.3 0.0 copy-start
  112.3 28.2 %all_to_all.24 = bf16[1,24,32,640]{3,2,0,1:T(8,128)(2,1)S(1)} all-to-all(bf16[1,24,32,640]{3,2,0,1:T(8,128)(2,1)S(1)} %bitcast.36), channel_id=1, replica_groups=mesh['dp'=4,'seq'=8] {'seq'}, dimensions={1} | all-to-all | bytes 1966080 | tf_op jit(solution)/shard_map/all_to_all | solution.py:57
  140.5 0.1 copy.46
  140.6 0.0 all-gather.5.cloned.1.call-done
  140.6 0.0 copy-done
  140.6 4.4 %fusion.3 = bf16[768,1280]{1,0:T(8,128)(2,1)} fusion(bf16[768,640]{1,0:T(8,128)(2,1)S(1)} %bitcast.39, bf16[640,1280]{0,1:T(8,128)(2,1)} %all-gather.5.cloned.1.call-done, bf16[768,1280]{1,0:T(8,128)(2,1)S(1)} %bitcast.38), kind=kOutput, calls=%fused_computation.7 | convolution fusion | flops 1261240320 | bytes 6553600 | tf_op jit(solution)/shard_map/dot_general | solution.py:64
  (4 shorter events, 0.0 us)
Async XLA Ops:
  6.5 78.9 %all-gather.3.cloned.1.call-start = ((), (), s32[]{:S(2)}) async-start(), calls=%async_computation.2 | async-start | bytes 6144000 | tf_op jit(solution)/shard_map/all_gather | solution.py:51
  12.0 8.2 %copy-start.2 = (s32[1,24]{1,0:T(1,128)S(1)}, s32[1,24]{1,0:T(1,128)}, u32[]{:S(2)}) copy-start(s32[1,24]{1,0:T(1,128)} %param.6) | copy-start | bytes 292
  12.0 66.9 %all-to-all-start = ((bf16[1,3,256,1280]{3,1,0,2:T(4,128)(2,1)}), bf16[1,3,256,1280]{3,1,0,2:T(4,128)(2,1)S(1)}, u32[]{:S(2)}, u32[]{:S(2)}) async-start(bf16[1,3,256,1280]{3,1,0,2:T(4,128)(2,1)} %copy.35), calls=%async_computation | async-start | bytes 5242880 | tf_op jit(solution)/shard_map/all_to_all | solution.py:43
  19.4 121.2 %all-gather.5.cloned.1.call-start = ((), (), s32[]{:S(2)}) async-start(), calls=%async_computation.3 | async-start | bytes 2048000 | tf_op jit(solution)/shard_map/all_gather | solution.py:66
  82.4 2.4 %copy-start.1 = (f32[1280]{0:T(1024)S(1)}, f32[1280]{0:T(1024)}, u32[]{:S(2)}) copy-start(f32[1280]{0:T(1024)} %param.7) | copy-start | bytes 15364
  112.3 28.3 %copy-start = (bf16[1,3,256,1280]{3,2,1,0:T(8,128)(2,1)S(1)}, bf16[1,3,256,1280]{3,2,1,0:T(8,128)(2,1)}, u32[]{:S(2)}) copy-start(bf16[1,3,256,1280]{3,2,1,0:T(8,128)(2,1)} %param.5) | copy-start | bytes 5898244
Sparse Core Ops, SparseCore 0:
  8.9 41.2 all-gather.2
  51.8 19.9 all-gather.4
where the time goes:
time: 152 us
  waiting for transfers between devices  60.1 us (40%)
  blocking collectives  28.2 us (19%)
  matrix products  22 us (14%)
  local copies, waits for them, and re-layouts  14.9 us (10%)
  between operations  13.6 us (9%)
  starting transfers between devices  7.45 us (5%)
  other arithmetic  5.69 us (4%)
    all_to_all x1, waiting for transfers between devices, shards(): lax.all_to_all(tokens, 'seq', split_axis=2, concat_axis=1, tiled=True)  58.6 us
    all_to_all x1, blocking collectives, shards(): lax.all_to_all(mixed.reshape(1, frames, places, HD), 'seq', split_axis=1,...  28.2 us
    dot_general x1, matrix products, column_block(): return jnp.dot(normed, piece, preferred_element_type=jnp.float32)  8.52 us
    all_to_all x1, starting transfers between devices, shards(): lax.all_to_all(tokens, 'seq', split_axis=2, concat_axis=1, tiled=True)  7.41 us
    dot_general x1, matrix products, attend(): jnp.einsum('flhe,glhe->lhfg', queries, keys, preferred_element_type=jnp.f...  5.69 us
    unnamed x7, local copies, waits for them, and re-layouts  4.77 us
    dot_general x1, matrix products, column_block(): return jnp.dot(rows_in, piece, preferred_element_type=jnp.float32)  4.43 us
    dot_general x1, matrix products, attend(): jnp.einsum('lhfg,glhe->flhe', attn_probs, values, preferred_element_type=...  3.4 us
  transfers between devices with their start and end apart: 3, of which 1 were waited for; matrix products, arithmetic and copies ran while one was open for 25% of the time, Pallas kernels for 0%

commit v1 on v0

--- a/solution.py
+++ b/solution.py
@@ -40,7 +40,19 @@
     frames = clip_row.shape[0]
     local_frames = tokens.shape[1]
     patches = tokens.shape[2]
-    moved = lax.all_to_all(tokens, "seq", split_axis=2, concat_axis=1, tiled=True)
+    ways, here = (lax.axis_size("seq"), lax.axis_index("seq"))
+    width_2 = tokens.shape[2] // ways
+    shape = list(tokens.shape)
+    shape[2] = width_2
+    height = shape[1]
+    shape[1] = height * ways
+    full = jnp.zeros(shape, tokens.dtype)
+    for mask in range(ways):
+        part = lax.dynamic_slice_in_dim(tokens, (here ^ mask) * width_2, width_2, axis=2)
+        if mask:
+            part = lax.ppermute(part, "seq", [(d, d ^ mask) for d in range(ways)])
+        full = lax.dynamic_update_slice_in_dim(full, part, (here ^ mask) * height, axis=1)
+    moved = full
     places = moved.shape[2]
     normed = layer_norm(moved, ln_gain).reshape(frames * places, width)
 

time: 152 us -> 132 us (0.87)
  waiting for transfers between devices: 60.1 us -> 29 us
  blocking collectives: 28.2 us -> 35 us
  starting transfers between devices: 7.45 us -> 13.7 us
  local copies, waits for them, and re-layouts: 14.9 us -> 11.9 us
    all_to_all x1 -> x0, waiting for transfers between devices: 58.6 us -> none  [shards(): lax.all_to_all(tokens, 'seq', split_axis=2, concat_axis=1, tiled=True)]
    ppermute x0 -> x7, waiting for transfers between devices: none -> 28.2 us  [shards(): part = lax.ppermute(part, 'seq', [(d, d ^ mask) for d in range(ways)])]
    ppermute x0 -> x7, starting transfers between devices: none -> 13.7 us  [shards(): part = lax.ppermute(part, 'seq', [(d, d ^ mask) for d in range(ways)])]
    all_to_all x1 -> x0, starting transfers between devices: 7.41 us -> none  [shards(): lax.all_to_all(tokens, 'seq', split_axis=2, concat_axis=1, tiled=True)]
    all_to_all x1, blocking collectives: 28.2 us -> 35 us  [shards(): lax.all_to_all(mixed.reshape(1, frames, places, HD), 'seq', split_axis=1,...]
    convert_element_type x1 -> x0, local copies, waits for them, and re-layouts: 2.42 us -> none  [layer_norm(): values = block.astype(jnp.float32)]
    convert_element_type x1 -> x0, other arithmetic: 2.34 us -> none  [layer_norm(): values = block.astype(jnp.float32)]
    unnamed x7 -> x8, local copies, waits for them, and re-layouts: 4.77 us -> 2.74 us
  transfers between devices with their start and end apart: 3 -> 9, of which waited for: 1 -> 4; matrix products, arithmetic and copies ran while one was open for 25% -> 25% of each run, Pallas kernels for 0% -> 0%
where the time goes in v1:
time: 132 us; the launch traced here: 131 us
  blocking collectives  35 us (27%)
  waiting for transfers between devices  29 us (22%)
  matrix products  23.4 us (18%)
  starting transfers between devices  13.7 us (10%)
  between operations  13.6 us (10%)
  local copies, waits for them, and re-layouts  11.9 us (9%)
  other arithmetic  4.72 us (4%)
    all_to_all x1, blocking collectives, shards(): lax.all_to_all(mixed.reshape(1, frames, places, HD), 'seq', split_axis=1,...  35 us
    ppermute x7, waiting for transfers between devices, shards(): part = lax.ppermute(part, 'seq', [(d, d ^ mask) for d in range(ways)])  28.2 us
    ppermute x7, starting transfers between devices, shards(): part = lax.ppermute(part, 'seq', [(d, d ^ mask) for d in range(ways)])  13.7 us
    dot_general x1, matrix products, column_block(): return jnp.dot(normed, piece, preferred_element_type=jnp.float32)  9.89 us
    dot_general x1, matrix products, attend(): jnp.einsum('flhe,glhe->lhfg', queries, keys, preferred_element_type=jnp.f...  5.66 us
    dot_general x1, matrix products, column_block(): return jnp.dot(rows_in, piece, preferred_element_type=jnp.float32)  4.43 us
    dot_general x1, matrix products, attend(): jnp.einsum('lhfg,glhe->flhe', attn_probs, values, preferred_element_type=...  3.41 us
    unnamed x8, local copies, waits for them, and re-layouts  2.74 us
  transfers between devices with their start and end apart: 9, of which 4 were waited for; matrix products, arithmetic and copies ran while one was open for 25% of the time, Pallas kernels for 0%

profile of v1, /device:TPU:0, one launch (start us, length us, event | category | flops | bytes accessed | tf_op | source)
XLA Modules:
  0.0 131.5 jit_solution(11793684833606108414)
XLA Ops:
  6.5 0.0 all-gather.3.cloned.1.call-start
  6.5 0.7 all-gather.3.cloned.1.call-update
  7.3 0.0 all-gather.5.cloned.1.call-start
  7.3 0.0 copy-start
  7.4 0.2 broadcast_in_dim.14
  7.6 1.3 %copy-done = bf16[1,3,256,1280]{3,2,1,0:T(8,128)(2,1)S(1)} copy-done((bf16[1,3,256,1280]{3,2,1,0:T(8,128)(2,1)S(1)}, bf16[1,3,256,1280]{3,2,1,0:T(8,128)(2,1)}, u32[]{:S(2)}) %copy-start) | copy-done | bytes 1966104
  8.9 0.0 copy-start.3
  8.9 1.1 constant_dynamic-slice_fusion
  10.0 3.0 %collective-permute-start = (bf16[1,3,32,1280]{3,2,1,0:T(8,128)(2,1)}, bf16[1,3,32,1280]{3,2,1,0:T(8,128)(2,1)S(1)}, u32[]{:S(2)}, u32[]{:S(2)}) collective-permute-start(bf16[1,3,32,1280]{3,2,1,0:T(8,128)(2,1)} %get-tuple-element.12), channel_id=1, source_target_pairs={{0,1},{1,0},{2,3},{3,2},{4,5},{5,4},{6,7},{7,6},{8,9},{9,8},{10,11... | collective-permute-start | bytes 737288 | tf_op jit(solution)/shard_map/ppermute | solution.py:53
  13.0 1.6 %collective-permute-start.1 = (bf16[1,3,32,1280]{3,2,1,0:T(8,128)(2,1)}, bf16[1,3,32,1280]{3,2,1,0:T(8,128)(2,1)S(1)}, u32[]{:S(2)}, u32[]{:S(2)}) collective-permute-start(bf16[1,3,32,1280]{3,2,1,0:T(8,128)(2,1)} %get-tuple-element.11), channel_id=1, source_target_pairs={{0,2},{1,3},{2,0},{3,1},{4,6},{5,7},{6,4},{7,5},{8,10},{9,11},{10,... | collective-permute-start | bytes 737288 | tf_op jit(solution)/shard_map/ppermute | solution.py:53
  14.6 0.0 collective-permute-start.2
  14.6 3.0 %collective-permute-start.3 = (bf16[1,3,32,1280]{3,2,1,0:T(8,128)(2,1)}, bf16[1,3,32,1280]{3,2,1,0:T(8,128)(2,1)S(1)}, u32[]{:S(2)}, u32[]{:S(2)}) collective-permute-start(bf16[1,3,32,1280]{3,2,1,0:T(8,128)(2,1)} %get-tuple-element.9), channel_id=1, source_target_pairs={{0,4},{1,5},{2,6},{3,7},{4,0},{5,1},{6,2},{7,3},{8,12},{9,13},{10,... | collective-permute-start | bytes 737288 | tf_op jit(solution)/shard_map/ppermute | solution.py:53
  17.6 1.3 collective-permute-start.4
  18.8 0.0 all-gather.5.cloned.1.call-update
  18.9 0.0 copy-done.3
  18.9 0.1 broadcast_compare_fusion
  18.9 0.2 collective-permute-done
  19.1 3.9 %collective-permute-start.5 = (bf16[1,3,32,1280]{3,2,1,0:T(8,128)(2,1)}, bf16[1,3,32,1280]{3,2,1,0:T(8,128)(2,1)S(1)}, u32[]{:S(2)}, u32[]{:S(2)}) collective-permute-start(bf16[1,3,32,1280]{3,2,1,0:T(8,128)(2,1)} %get-tuple-element.14), channel_id=1, source_target_pairs={{0,6},{1,7},{2,4},{3,5},{4,2},{5,3},{6,0},{7,1},{8,14},{9,15},{10,... | collective-permute-start | bytes 737288 | tf_op jit(solution)/shard_map/ppermute | solution.py:53
  23.0 8.6 %collective-permute-done.1 = bf16[1,3,32,1280]{3,2,1,0:T(8,128)(2,1)S(1)} collective-permute-done((bf16[1,3,32,1280]{3,2,1,0:T(8,128)(2,1)}, bf16[1,3,32,1280]{3,2,1,0:T(8,128)(2,1)S(1)}, u32[]{:S(2)}, u32[]{:S(2)}) %collective-permute-start.1) | collective-permute-done | bytes 245792 | tf_op jit(solution)/shard_map/ppermute | solution.py:53
  31.6 1.0 collective-permute-start.6
  32.7 2.0 %collective-permute-done.2 = bf16[1,3,32,1280]{3,2,1,0:T(8,128)(2,1)S(1)} collective-permute-done((bf16[1,3,32,1280]{3,2,1,0:T(8,128)(2,1)}, bf16[1,3,32,1280]{3,2,1,0:T(8,128)(2,1)S(1)}, u32[]{:S(2)}, u32[]{:S(2)}) %collective-permute-start.2) | collective-permute-done | bytes 245792 | tf_op jit(solution)/shard_map/ppermute | solution.py:53
  34.7 0.0 collective-permute-done.3
  34.7 17.5 %collective-permute-done.4 = bf16[1,3,32,1280]{3,2,1,0:T(8,128)(2,1)S(1)} collective-permute-done((bf16[1,3,32,1280]{3,2,1,0:T(8,128)(2,1)}, bf16[1,3,32,1280]{3,2,1,0:T(8,128)(2,1)S(1)}, u32[]{:S(2)}, u32[]{:S(2)}) %collective-permute-start.4) | collective-permute-done | bytes 245792 | tf_op jit(solution)/shard_map/ppermute | solution.py:53
  52.2 0.0 collective-permute-done.5
  52.2 0.0 collective-permute-done.6
  52.3 0.0 copy-start.2
  52.3 0.3 convert_reduce_fusion
  52.6 0.7 fusion.2
  53.3 0.0 copy-done.2
  53.3 1.9 %fusion.4 = bf16[1,24,32,1280]{3,2,1,0:T(8,128)(2,1)} fusion(bf16[1,24,32,1280]{3,2,1,0:T(8,128)(2,1)S(1)} %constant_dynamic-update-slice_fusion.6, f32[1280]{0:T(1024)S(1)} %copy-done.2, f32[24,32]{1,0:T(8,128)S(1)} %add_rsqrt_fusion, f32[24,32]{1,0:T(8,128)S(1)} %broadcast_multiply_fusion), kind=kLoop, calls=%fused_computation.7 | loop fusion | flops 4915200 | bytes 3943424 | tf_op jit(solution)/shard_map/convert_element_type | solution.py:17
  55.2 0.0 all-gather.3.cloned.1.call-done
  55.2 9.9 %fusion.19 = (bf16[768,1920]{1,0:T(8,128)(2,1)S(1)}, f32[768,1920]{1,0:T(8,128)}) fusion(bf16[768,1280]{1,0:T(8,128)(2,1)} %bitcast.21, bf16[1280,1920]{0,1:T(8,128)(2,1)} %all-gather.3.cloned.1.call-done), kind=kOutput, calls=%fused_computation.42 | convolution fusion | flops 3776348160 | bytes 15728640 | tf_op jit(solution)/shard_map/dot_general | solution.py:60
  65.1 0.2 fusion.18
  65.3 1.8 %reshape.55 = bf16[24,32,8,80]{3,2,1,0:T(8,128)(2,1)S(1)} reshape(bf16[768,640]{1,0:T(8,128)(2,1)S(1)} %get-tuple-element.6) | data formatting | bytes 1966080 | tf_op jit(solution)/shard_map/reshape | solution.py:67
  67.1 1.7 %fusion.7 = bf16[768,640]{1,0:T(8,128)(2,1)S(1)} fusion(f32[768,1920]{1,0:T(8,128)} %get-tuple-element.16), kind=kLoop, calls=%fused_computation.13 | loop fusion | flops 983040 | bytes 2949120 | tf_op jit(solution)/shard_map/convert_element_type | solution.py:21
  68.8 2.5 %reshape.54 = bf16[24,32,8,80]{3,2,1,0:T(8,128)(2,1)} reshape(bf16[768,640]{1,0:T(8,128)(2,1)S(1)} %fusion.7) | data formatting | bytes 1966080 | tf_op jit(solution)/shard_map/reshape | solution.py:67
  71.3 5.7 %fusion.6 = (f32[32,8,24]{2,1,0:T(8,128)S(1)}, f32[32,8,24,24]{2,3,1,0:T(8,128)}) fusion(pred[24,24]{0,1:T(8,128)(4,1)S(1)} %broadcast_compare_fusion, bf16[24,32,8,80]{3,2,1,0:T(8,128)(2,1)S(1)} %reshape.55, bf16[24,32,8,80]{3,2,1,0:T(8,128)(2,1)} %reshape.54), kind=kOutput, calls=%fused_computation.11 | convolution fusion | flops 23881728 | bytes 2581056 | tf_op jit(solution)/shard_map/flhe,glhe->lhfg/dot_general | solution.py:28
  77.0 1.6 %reshape.53 = bf16[24,32,8,80]{3,2,1,0:T(8,128)(2,1)S(1)} reshape(bf16[768,640]{1,0:T(8,128)(2,1)S(1)} %get-tuple-element.5) | data formatting | bytes 1966080 | tf_op jit(solution)/shard_map/reshape | solution.py:67
  78.6 3.4 %fusion.14 = bf16[24,32,8,80]{3,0,2,1:T(8,128)(2,1)S(1)} fusion(f32[32,8,24,24]{2,3,1,0:T(8,128)} %get-tuple-element.18, f32[32,8,24]{2,1,0:T(8,128)S(1)} %get-tuple-element.17, pred[24,24]{0,1:T(8,128)(4,1)S(1)} %broadcast_compare_fusion, bf16[24,32,8,80]{3,2,1,0:T(8,128)(2,1)S(1)} %reshape.53), kind=kOutput, calls=%fused_computation.21 | convolution fusion | flops 24526848 | bytes 2581056 | tf_op jit(solution)/shard_map/lhfg,glhe->flhe/dot_general | solution.py:32
  82.0 0.3 copy.26
  82.4 1.2 reshape.56
  83.6 35.0 %all_to_all.15 = bf16[1,24,32,640]{3,2,0,1:T(8,128)(2,1)S(1)} all-to-all(bf16[1,24,32,640]{3,2,0,1:T(8,128)(2,1)S(1)} %bitcast.18), channel_id=1, replica_groups=mesh['dp'=4,'seq'=8] {'seq'}, dimensions={1} | all-to-all | bytes 1966080 | tf_op jit(solution)/shard_map/all_to_all | solution.py:69
  118.6 0.0 copy-start.1
  118.6 0.1 copy.28
  118.8 0.0 all-gather.5.cloned.1.call-done
  118.8 1.4 %copy-done.1 = bf16[1,3,256,1280]{3,2,1,0:T(8,128)(2,1)S(1)} copy-done((bf16[1,3,256,1280]{3,2,1,0:T(8,128)(2,1)S(1)}, bf16[1,3,256,1280]{3,2,1,0:T(8,128)(2,1)}, u32[]{:S(2)}) %copy-start.1) | copy-done | bytes 1966104
  120.2 4.4 %fusion.5 = bf16[768,1280]{1,0:T(8,128)(2,1)} fusion(bf16[768,640]{1,0:T(8,128)(2,1)S(1)} %bitcast.22, bf16[640,1280]{0,1:T(8,128)(2,1)} %all-gather.5.cloned.1.call-done, bf16[768,1280]{1,0:T(8,128)(2,1)S(1)} %bitcast.20), kind=kOutput, calls=%fused_computation.8 | convolution fusion | flops 1261240320 | bytes 6553600 | tf_op jit(solution)/shard_map/dot_general | solution.py:76
  (9 shorter events, 0.2 us)
Async XLA Ops:
  6.5 48.7 %all-gather.3.cloned.1.call-start = ((), (), s32[]{:S(2)}) async-start(), calls=%async_computation.1 | async-start | bytes 6144000 | tf_op jit(solution)/shard_map/all_gather | solution.py:63
  7.3 111.5 %all-gather.5.cloned.1.call-start = ((), (), s32[]{:S(2)}) async-start(), calls=%async_computation.2 | async-start | bytes 2048000 | tf_op jit(solution)/shard_map/all_gather | solution.py:78
  7.3 1.5 %copy-start = (bf16[1,3,256,1280]{3,2,1,0:T(8,128)(2,1)S(1)}, bf16[1,3,256,1280]{3,2,1,0:T(8,128)(2,1)}, u32[]{:S(2)}) copy-start(bf16[1,3,256,1280]{3,2,1,0:T(8,128)(2,1)} %param.5) | copy-start | bytes 5898244
  8.9 10.0 %copy-start.3 = (s32[1,24]{1,0:T(1,128)S(1)}, s32[1,24]{1,0:T(1,128)}, u32[]{:S(2)}) copy-start(s32[1,24]{1,0:T(1,128)} %param.6) | copy-start | bytes 292
  10.0 9.1 %collective-permute-start = (bf16[1,3,32,1280]{3,2,1,0:T(8,128)(2,1)}, bf16[1,3,32,1280]{3,2,1,0:T(8,128)(2,1)S(1)}, u32[]{:S(2)}, u32[]{:S(2)}) collective-permute-start(bf16[1,3,32,1280]{3,2,1,0:T(8,128)(2,1)} %get-tuple-element.12), channel_id=1, source_target_pairs={{0,1},{1,0},{2,3},{3,2},{4,5},{5,4},{6,7},{7,6},{8,9},{9,8},{10,11... | collective-permute-start | bytes 737288 | tf_op jit(solution)/shard_map/ppermute | solution.py:53
  13.0 18.6 %collective-permute-start.1 = (bf16[1,3,32,1280]{3,2,1,0:T(8,128)(2,1)}, bf16[1,3,32,1280]{3,2,1,0:T(8,128)(2,1)S(1)}, u32[]{:S(2)}, u32[]{:S(2)}) collective-permute-start(bf16[1,3,32,1280]{3,2,1,0:T(8,128)(2,1)} %get-tuple-element.11), channel_id=1, source_target_pairs={{0,2},{1,3},{2,0},{3,1},{4,6},{5,7},{6,4},{7,5},{8,10},{9,11},{10,... | collective-permute-start | bytes 737288 | tf_op jit(solution)/shard_map/ppermute | solution.py:53
  14.6 20.1 %collective-permute-start.2 = (bf16[1,3,32,1280]{3,2,1,0:T(8,128)(2,1)}, bf16[1,3,32,1280]{3,2,1,0:T(8,128)(2,1)S(1)}, u32[]{:S(2)}, u32[]{:S(2)}) collective-permute-start(bf16[1,3,32,1280]{3,2,1,0:T(8,128)(2,1)} %get-tuple-element.10), channel_id=1, source_target_pairs={{0,3},{1,2},{2,1},{3,0},{4,7},{5,6},{6,5},{7,4},{8,11},{9,10},{10,... | collective-permute-start | bytes 737288 | tf_op jit(solution)/shard_map/ppermute | solution.py:53
  14.6 20.1 %collective-permute-start.3 = (bf16[1,3,32,1280]{3,2,1,0:T(8,128)(2,1)}, bf16[1,3,32,1280]{3,2,1,0:T(8,128)(2,1)S(1)}, u32[]{:S(2)}, u32[]{:S(2)}) collective-permute-start(bf16[1,3,32,1280]{3,2,1,0:T(8,128)(2,1)} %get-tuple-element.9), channel_id=1, source_target_pairs={{0,4},{1,5},{2,6},{3,7},{4,0},{5,1},{6,2},{7,3},{8,12},{9,13},{10,... | collective-permute-start | bytes 737288 | tf_op jit(solution)/shard_map/ppermute | solution.py:53
  17.6 34.6 %collective-permute-start.4 = (bf16[1,3,32,1280]{3,2,1,0:T(8,128)(2,1)}, bf16[1,3,32,1280]{3,2,1,0:T(8,128)(2,1)S(1)}, u32[]{:S(2)}, u32[]{:S(2)}) collective-permute-start(bf16[1,3,32,1280]{3,2,1,0:T(8,128)(2,1)} %get-tuple-element.8), channel_id=1, source_target_pairs={{0,5},{1,4},{2,7},{3,6},{4,1},{5,0},{6,3},{7,2},{8,13},{9,12},{10,... | collective-permute-start | bytes 737288 | tf_op jit(solution)/shard_map/ppermute | solution.py:53
  19.1 33.1 %collective-permute-start.5 = (bf16[1,3,32,1280]{3,2,1,0:T(8,128)(2,1)}, bf16[1,3,32,1280]{3,2,1,0:T(8,128)(2,1)S(1)}, u32[]{:S(2)}, u32[]{:S(2)}) collective-permute-start(bf16[1,3,32,1280]{3,2,1,0:T(8,128)(2,1)} %get-tuple-element.14), channel_id=1, source_target_pairs={{0,6},{1,7},{2,4},{3,5},{4,2},{5,3},{6,0},{7,1},{8,14},{9,15},{10,... | collective-permute-start | bytes 737288 | tf_op jit(solution)/shard_map/ppermute | solution.py:53
  31.6 20.6 %collective-permute-start.6 = (bf16[1,3,32,1280]{3,2,1,0:T(8,128)(2,1)S(1)}, bf16[1,3,32,1280]{3,2,1,0:T(8,128)(2,1)S(1)}, u32[]{:S(2)}, u32[]{:S(2)}) collective-permute-start(bf16[1,3,32,1280]{3,2,1,0:T(8,128)(2,1)S(1)} %get-tuple-element.7), channel_id=1, source_target_pairs={{0,7},{1,6},{2,5},{3,4},{4,3},{5,2},{6,1},{7,0},{8,15},{9,14},{10,... | collective-permute-start | bytes 737288 | tf_op jit(solution)/shard_map/ppermute | solution.py:53
  52.3 1.0 copy-start.2
  118.6 1.5 %copy-start.1 = (bf16[1,3,256,1280]{3,2,1,0:T(8,128)(2,1)S(1)}, bf16[1,3,256,1280]{3,2,1,0:T(8,128)(2,1)}, u32[]{:S(2)}) copy-start(bf16[1,3,256,1280]{3,2,1,0:T(8,128)(2,1)} %param.5) | copy-start | bytes 5898244
Sparse Core Ops, SparseCore 0:
  8.9 41.2 all-gather.2
  51.8 19.9 all-gather.4
